TPU v7x, 512 devices: a whole 4x4x16 slice. The times are simulated.
512 devices in a mesh: rep: 4 (over x), fsdp: 16 (over z), tp: 8 (over y, core).
Axes of the slice: x: 4, y: 4, z: 16, core: 2. Of those that a mesh axis runs over, the one named last changes fastest.
Arguments:
- tracker: bfloat16 [4, 4096, 14336], P('rep', 'fsdp', 'tp'), may hold values from -20 to 20
- grad_delta: bfloat16 [4, 4096, 14336], P('rep', 'fsdp', 'tp'), may hold values from -20 to 20
- momentum: bfloat16 [4, 4096, 14336], P('rep', 'fsdp', 'tp'), may hold values from -20 to 20
- q_basis: bfloat16 [4, 14336, 512], P('rep', 'tp', 'fsdp'), may hold values from -0.046875 to 0.046875
- mix_counts: int32 [4, 3], replicated, may hold values from 1 to 8
Outputs:
- new_tracker: bfloat16 [4, 4096, 14336], P('rep', 'fsdp', 'tp')
- new_momentum: bfloat16 [4, 4096, 14336], P('rep', 'fsdp', 'tp')
- left_basis: bfloat16 [4, 4096, 512], P('rep', 'fsdp')
- q_new: bfloat16 [4, 14336, 512], P('rep', 'tp', 'fsdp')
All inputs are finite; a program needn't handle non-finite values.
Results may differ from a plain program's by a relative error of at most 0.0061.
Values may be sent and summed in bfloat16 or wider, within the bound.
A program may use at most 64 MiB of HBM per device.

v0:
```python
import jax
import jax.numpy as jnp
from jax import lax
from jax.sharding import PartitionSpec as P

D = 4096
FF = 14336


def extended(block, sides, width):
    for axis, dim in sides:
        count = lax.axis_size(axis)
        forward = [(i, i + 1) for i in range(count - 1)]
        forward.append((count - 1, 0))
        backward = [(target, source) for source, target in forward]
        low = lax.ppermute(
            lax.slice_in_dim(block, block.shape[dim] - width, None, axis=dim), axis, forward
        )
        high = lax.ppermute(lax.slice_in_dim(block, 0, width, axis=dim), axis, backward)
        block = jnp.concatenate([low, block, high], axis=dim)
    return block


def orthonormal(pmat, gram):
    factor = jnp.linalg.cholesky(gram)
    solved = jax.scipy.linalg.solve_triangular(factor, pmat.T, lower=True).T
    return (solved * jnp.sqrt(jnp.float32(D))).astype(jnp.bfloat16)


def local(tracker, grad_delta, momentum, q_basis, mix_counts):
    agent = lax.axis_index("rep")
    counts = mix_counts.astype(jnp.float32)
    select = (jnp.arange(counts.shape[0]) == agent).astype(jnp.float32)
    mine = jnp.sum(select[:, None] * counts, axis=0)
    weights = mine / jnp.sum(mine)
    near = extended(tracker, (("rep", 0),), 1)
    mixed = (
        weights[0] * near[1].astype(jnp.float32)
        + weights[1] * near[0].astype(jnp.float32)
        + weights[2] * near[2].astype(jnp.float32)
    )
    tracked = mixed + grad_delta[0].astype(jnp.float32)
    new_tracker = tracked.astype(jnp.bfloat16)
    accum = momentum[0].astype(jnp.float32) + tracked
    accum_b = accum.astype(jnp.bfloat16)
    scale = 1.0 / jnp.sqrt(jnp.float32(D))
    basis_full = lax.all_gather(q_basis, "fsdp", axis=2, tiled=True)[0]
    partial_left = jnp.dot(accum_b, basis_full, preferred_element_type=jnp.float32)
    pmat = lax.psum(partial_left, "tp")
    gram_part = jnp.dot(pmat.T, pmat, precision=lax.Precision.HIGHEST)
    gram = lax.psum(gram_part, "fsdp")
    left_b = orthonormal(pmat, gram)
    block = left_b
    product = lax.dot_general(
        block, accum_b, (((0,), (0,)), ((), ())), preferred_element_type=jnp.float32
    )
    right_t = lax.psum_scatter(product * scale, "fsdp", scatter_dimension=0, tiled=True)
    squares = lax.psum(jnp.sum(right_t * right_t, axis=1), "tp")
    rms = jnp.sqrt(squares / FF) + 1e-06
    q_new = (right_t / rms[:, None]).T.astype(jnp.bfloat16)
    right_b = right_t.astype(jnp.bfloat16)
    block = left_b
    feed = jnp.dot(
        block,
        lax.all_gather(right_b, "fsdp", axis=0, tiled=True),
        preferred_element_type=jnp.float32,
    )
    new_momentum = (accum - 0.5 * scale * feed).astype(jnp.bfloat16)
    return (new_tracker[None], new_momentum[None], left_b[None], q_new[None])


def solution(mesh):
    in_specs = (
        P("rep", "fsdp", "tp"),
        P("rep", "fsdp", "tp"),
        P("rep", "fsdp", "tp"),
        P("rep", "tp", "fsdp"),
        P(),
    )
    out_specs = (
        P("rep", "fsdp", "tp"),
        P("rep", "fsdp", "tp"),
        P("rep", "fsdp", None),
        P("rep", "tp", "fsdp"),
    )
    return jax.shard_map(local, mesh=mesh, in_specs=in_specs, out_specs=out_specs, check_vma=False)
```

profile of v0, /device:TPU:2, one launch (start us, length us, event | category | flops | bytes accessed | tf_op | source)
XLA Modules:
  0.0 640.5 jit_solution(14598845073682928262)
XLA Ops:
  7.2 0.7 all-gather.3.cloned.1.call-update
  7.9 7.8 %collective-permute-start.1 = (bf16[1,256,1792]{2,1,0:T(8,128)(2,1)}, bf16[1,256,1792]{2,1,0:T(8,128)(2,1)S(1)}, u32[]{:S(2)}, u32[]{:S(2)}) collective-permute-start(bf16[1,256,1792]{2,1,0:T(8,128)(2,1)} %param.5), channel_id=1, source_target_pairs={{128,0},{256,128},{384,256},{0,384},{129,1},{257,129},{385,257},{1... | collective-permute-start | bytes 2752520 | tf_op jit(solution)/shard_map/ppermute | solution.py:19
  15.8 1.9 collective-permute-start
  17.7 1.4 fusion.37
  19.1 0.6 broadcast_divide_fusion
  19.7 0.6 fusion.46
  20.3 11.8 %collective-permute-done.1 = bf16[1,256,1792]{2,1,0:T(8,128)(2,1)S(1)} collective-permute-done((bf16[1,256,1792]{2,1,0:T(8,128)(2,1)}, bf16[1,256,1792]{2,1,0:T(8,128)(2,1)S(1)}, u32[]{:S(2)}, u32[]{:S(2)}) %collective-permute-start.1) | collective-permute-done | bytes 917536 | tf_op jit(solution)/shard_map/ppermute | solution.py:19
  32.1 3.2 collective-permute-done
  35.3 0.9 copy-done.6
  36.3 5.5 fusion.44
  41.8 45.7 %all-gather.3.cloned.1.call-done = bf16[1,1792,512]{1,2,0:T(8,128)(2,1)} async-done(((bf16[1,1792,32]{1,2,0:T(8,128)(2,1)}), bf16[1,1792,512]{1,2,0:T(8,128)(2,1)}) %all-gather.3.cloned.1.call-update) | async-done | bytes 1835024 | tf_op jit(solution)/shard_map/all_gather | solution.py:47
  87.5 3.0 fusion.3
  90.6 73.0 %all-reduce.4.cloned.1.call-done = f32[256,512]{1,0:T(8,128)} async-done(((f32[256,512]{1,0:T(8,128)}), f32[256,512]{1,0:T(8,128)}) %all-reduce.4.cloned.1.call-update) | async-done | bytes 524304 | tf_op jit(solution)/shard_map/psum | solution.py:49
  163.6 3.3 fusion.47
  167.1 138.0 %all-reduce.6.cloned.1.call-done = f32[512,512]{0,1:T(8,128)} async-done(((f32[512,512]{0,1:T(8,128)}), f32[512,512]{0,1:T(8,128)}) %all-reduce.6.cloned.1.call-update) | async-done | bytes 1048592 | tf_op jit(solution)/shard_map/psum | solution.py:51
  305.1 2.6 copy.10
  307.7 1.8 fusion.5
  309.5 1.0 copy-done.4
  310.5 11.7 %cholesky.104 = f32[128,128]{1,0:T(8,128)S(1)} custom-call(f32[128,128]{1,0:T(8,128)S(1)} %cholesky.266), custom_call_target="Cholesky" | custom-call | tf_op jit(solution)/shard_map/jit(cholesky)/cholesky | solution.py:25
  322.2 1.2 cholesky.224
  323.4 9.8 %custom-call.31 = f32[1,128,128]{1,2,0:T(8,128)S(1)} custom-call(f32[1,128,128]{2,1,0:T(8,128)S(1)} %get-tuple-element.41), custom_call_target="InvertDiagBlocksLowerTriangular" | custom-call | tf_op jit(solution)/shard_map/jit(cholesky)/cholesky | solution.py:25
  333.2 2.0 constant_dynamic-update-slice_fusion.3
  335.2 1.2 convolution_subtract_fusion
  336.5 11.7 %cholesky.217 = f32[128,128]{1,0:T(8,128)S(1)} custom-call(f32[128,128]{1,0:T(8,128)S(1)} %cholesky.270), custom_call_target="Cholesky" | custom-call | tf_op jit(solution)/shard_map/jit(cholesky)/cholesky | solution.py:25
  348.2 0.6 select_reduce_fusion.2
  348.8 10.0 %custom-call.32 = f32[1,128,128]{1,2,0:T(8,128)S(1)} custom-call(f32[1,128,128]{2,1,0:T(8,128)S(1)} %get-tuple-element.38), custom_call_target="InvertDiagBlocksLowerTriangular" | custom-call | tf_op jit(solution)/shard_map/jit(cholesky)/cholesky | solution.py:25
  358.8 0.9 convolution_dynamic-update-slice_fusion
  359.8 1.4 convolution_subtract_fusion.3
  361.2 11.7 %cholesky.238 = f32[128,128]{1,0:T(8,128)S(1)} custom-call(f32[128,128]{1,0:T(8,128)S(1)} %cholesky.275), custom_call_target="Cholesky" | custom-call | tf_op jit(solution)/shard_map/jit(cholesky)/cholesky | solution.py:25
  372.9 0.6 select_reduce_fusion.1
  373.6 9.8 %custom-call.33 = f32[1,128,128]{1,2,0:T(8,128)S(1)} custom-call(f32[1,128,128]{2,1,0:T(8,128)S(1)} %get-tuple-element.35), custom_call_target="InvertDiagBlocksLowerTriangular" | custom-call | tf_op jit(solution)/shard_map/jit(cholesky)/cholesky | solution.py:25
  383.4 0.8 convolution_dynamic-update-slice_fusion.1
  384.2 1.4 convolution_subtract_fusion.5
  385.6 11.7 %cholesky.255 = f32[128,128]{1,0:T(8,128)S(1)} custom-call(f32[128,128]{1,0:T(8,128)S(1)} %convolution_subtract_fusion.5), custom_call_target="Cholesky" | custom-call | tf_op jit(solution)/shard_map/jit(cholesky)/cholesky | solution.py:25
  397.3 0.7 select_reduce_fusion
  398.0 0.7 compare_reduce_fusion.1
  398.7 0.6 compare_reduce_fusion
  399.3 0.7 compare_reduce_fusion.2
  402.5 2.6 select_select_fusion
  405.1 14.5 %while.1 = (s32[]{:T(128)}, f32[512,512]{1,0:T(8,128)}, s32[4,2]{0,1:T(2,128)S(1)}, f32[4,128,128]{2,1,0:T(8,128)}, s32[]{:T(128)}) while((s32[]{:T(128)}, f32[512,512]{1,0:T(8,128)}, s32[4,2]{0,1:T(2,128)S(1)}, f32[4,128,128]{2,1,0:T(8,128)}, s32[]{:T(128)}) %tuple.37), condition=%wide.while_cond, body=%wide.while_body.sunk | while | flops 2 | bytes 132205 | solution.py:26
  405.2 0.6 fusion.57
  405.8 3.0 bitcast_dynamic-update-slice_fusion.2
  408.9 0.6 fusion.57
  409.4 3.0 bitcast_dynamic-update-slice_fusion.2
  412.5 0.6 fusion.57
  413.1 3.0 bitcast_dynamic-update-slice_fusion.2
  416.1 0.6 fusion.57
  416.7 2.9 bitcast_dynamic-update-slice_fusion.2
  419.6 40.8 %custom-call.34 = f32[4,128,128]{1,2,0:T(8,128)} custom-call(f32[4,128,128]{2,1,0:T(8,128)} %get-tuple-element.11), custom_call_target="InvertDiagBlocksLowerTriangular" | custom-call | tf_op jit(solution)/shard_map/jit(_solve_triangular)/triangular_solve | solution.py:26
  460.4 1.1 fusion.23
  461.5 1.2 convolution_subtract_fusion.4
  462.8 1.2 fusion.31
  463.9 1.5 convolution_subtract_fusion.2
  465.4 1.2 fusion.29
  466.6 1.8 convolution_subtract_fusion.1
  468.4 1.2 fusion.28
  469.6 2.5 convolution_multiply_fusion
  472.1 75.2 %reduce-scatter.2.cloned.1.call-done = f32[32,1792]{1,0:T(8,128)} async-done(((f32[512,1792]{1,0:T(8,128)}), f32[32,1792]{1,0:T(8,128)}) %reduce-scatter.2.cloned.1.call-update) | async-done | bytes 229392 | tf_op jit(solution)/shard_map/reduce_scatter | solution.py:57
  547.3 1.1 multiply_reduce_fusion
  548.4 12.4 %psum.23 = f32[32]{0:T(128)S(1)} all-reduce(f32[32]{0:T(128)S(1)} %multiply_reduce_fusion), channel_id=1, replica_groups=mesh['rep'=4,'fsdp'=16,'tp'=8] {'tp'}, use_global_device_ids=true, to_apply=%region_14.15 | all-reduce | flops 32 | bytes 256 | tf_op jit(solution)/shard_map/psum | solution.py:58
  560.8 1.8 fusion.27
  562.7 0.8 copy.11
  563.5 67.4 %all-gather.5.cloned.1.call-done = bf16[512,1792]{1,0:T(8,128)(2,1)} async-done(((bf16[32,1792]{1,0:T(8,128)(2,1)}), bf16[512,1792]{1,0:T(8,128)(2,1)}) %all-gather.5.cloned.1.call-update) | async-done | bytes 1835024 | tf_op jit(solution)/shard_map/all_gather | solution.py:65
  630.9 3.1 fusion.2
  (35 shorter events, 0.9 us)
Async XLA Ops:
  7.2 80.3 %all-gather.3.cloned.1.call-start = ((), (), s32[]{:S(2)}) async-start(), calls=%async_computation.1 | async-start | bytes 1949696 | tf_op jit(solution)/shard_map/all_gather | solution.py:47
  7.9 155.7 %all-reduce.4.cloned.1.call-start = ((), (), s32[]{:S(2)}) async-start(), calls=%async_computation.2 | async-start | bytes 1048576 | tf_op jit(solution)/shard_map/psum | solution.py:49
  7.9 24.2 %collective-permute-start.1 = (bf16[1,256,1792]{2,1,0:T(8,128)(2,1)}, bf16[1,256,1792]{2,1,0:T(8,128)(2,1)S(1)}, u32[]{:S(2)}, u32[]{:S(2)}) collective-permute-start(bf16[1,256,1792]{2,1,0:T(8,128)(2,1)} %param.5), channel_id=1, source_target_pairs={{128,0},{256,128},{384,256},{0,384},{129,1},{257,129},{385,257},{1... | collective-permute-start | bytes 2752520 | tf_op jit(solution)/shard_map/ppermute | solution.py:19
  15.8 19.6 %collective-permute-start = (bf16[1,256,1792]{2,1,0:T(8,128)(2,1)}, bf16[1,256,1792]{2,1,0:T(8,128)(2,1)S(1)}, u32[]{:S(2)}, u32[]{:S(2)}) collective-permute-start(bf16[1,256,1792]{2,1,0:T(8,128)(2,1)} %param.5), channel_id=1, source_target_pairs={{0,128},{128,256},{256,384},{384,0},{1,129},{129,257},{257,385},{3... | collective-permute-start | bytes 2752520 | tf_op jit(solution)/shard_map/ppermute | solution.py:16
  32.1 3.2 copy-start.5
  35.3 0.9 copy-start.6
  36.3 51.2 %copy-start = (bf16[1,256,1792]{2,1,0:T(8,128)(2,1)S(1)}, bf16[1,256,1792]{2,1,0:T(8,128)(2,1)}, u32[]{:S(2)}) copy-start(bf16[1,256,1792]{2,1,0:T(8,128)(2,1)} %param.7) | copy-start | bytes 2752516
  90.5 214.6 %all-reduce.6.cloned.1.call-start = ((), (), s32[]{:S(2)}) async-start(), calls=%async_computation.3 | async-start | bytes 2097152 | tf_op jit(solution)/shard_map/psum | solution.py:51
  166.9 380.4 %reduce-scatter.2.cloned.1.call-start = ((), (), s32[]{:S(2)}) async-start(), calls=%async_computation.4 | async-start | bytes 3899392 | tf_op jit(solution)/shard_map/reduce_scatter | solution.py:57
  309.5 1.0 copy-start.4
  373.6 86.8 %copy-start.1 = (f32[256,512]{1,0:T(8,128)S(1)}, f32[256,512]{1,0:T(8,128)}, u32[]{:S(2)}) copy-start(f32[256,512]{1,0:T(8,128)} %all-reduce.4.cloned.1.call-done) | copy-start | bytes 1572868
  466.6 3.0 copy-start.2
  472.0 90.6 %copy-start.3 = (f32[128,256]{1,0:T(8,128)S(1)}, f32[128,256]{1,0:T(8,128)}, u32[]{:S(2)}) copy-start(f32[128,256]{1,0:T(8,128)} %copy-done.2) | copy-start | bytes 393220
  472.1 158.8 %all-gather.5.cloned.1.call-start = ((), (), s32[]{:S(2)}) async-start(), calls=%async_computation.5 | async-start | bytes 1949696 | tf_op jit(solution)/shard_map/all_gather | solution.py:65
Sparse Core Ops, SparseCore 0:
  10.1 77.3 all-gather.2
  90.6 72.8 all-reduce.3
  167.0 138.0 all-reduce.5
  472.2 75.0 reduce-scatter.1
  562.7 68.1 all-gather.4
where the time goes:
time: 642 us; the launch traced here: 641 us
  waiting for transfers between devices  415 us (65%)
  other arithmetic  136 us (21%)
  matrix products  28.8 us (4%)
  local copies, waits for them, and re-layouts  21.6 us (3%)
  between operations  16.5 us (3%)
  blocking collectives  12.4 us (2%)
  starting transfers between devices  10.1 us (2%)
    psum x1, waiting for transfers between devices, local(): gram = lax.psum(gram_part, 'fsdp')  138 us
    another operation x14, other arithmetic, orthonormal(): factor = jnp.linalg.cholesky(gram)  80.4 us
    reduce_scatter x1, waiting for transfers between devices, local(): lax.psum_scatter(product * scale, 'fsdp', scatter_dimension=0, tiled=True)  75.2 us
    psum x1, waiting for transfers between devices, local(): pmat = lax.psum(partial_left, 'tp')  73 us
    all_gather x1, waiting for transfers between devices, local(): lax.all_gather(right_b, 'fsdp', axis=0, tiled=True)  67.4 us
    all_gather x1, waiting for transfers between devices, local(): basis_full = lax.all_gather(q_basis, 'fsdp', axis=2, tiled=True)[0]  45.7 us
    another operation x3, other arithmetic, orthonormal(): solved = jax.scipy.linalg.solve_triangular(factor, pmat.T, lower=True).T  43.4 us
    another operation x12, local copies, waits for them, and re-layouts  14.5 us
  transfers between devices with their start and end apart: 7, of which 7 were waited for; matrix products, arithmetic and copies ran while one was open for 1% of the time, Pallas kernels for 0%

commit v1 on v0

--- a/solution.py
+++ b/solution.py
@@ -5,6 +5,11 @@
 
 D = 4096
 FF = 14336
+
+
+def gather_over(x, axis, d):
+    repeated = jnp.stack([x] * lax.axis_size(axis))
+    return jnp.concatenate(lax.all_to_all(repeated, axis, 0, 0), axis=d)
 
 
 def extended(block, sides, width):
@@ -44,7 +49,7 @@
     accum = momentum[0].astype(jnp.float32) + tracked
     accum_b = accum.astype(jnp.bfloat16)
     scale = 1.0 / jnp.sqrt(jnp.float32(D))
-    basis_full = lax.all_gather(q_basis, "fsdp", axis=2, tiled=True)[0]
+    basis_full = gather_over(q_basis, "fsdp", 2)[0]
     partial_left = jnp.dot(accum_b, basis_full, preferred_element_type=jnp.float32)
     pmat = lax.psum(partial_left, "tp")
     gram_part = jnp.dot(pmat.T, pmat, precision=lax.Precision.HIGHEST)

time: 642 us -> 664 us (1.034)
  starting transfers between devices: 10.1 us -> 21.6 us
  waiting for transfers between devices: 415 us -> 424 us
    all_to_all x0 -> x1, waiting for transfers between devices: none -> 51.9 us  [gather_over(): return jnp.concatenate(lax.all_to_all(repeated, axis, 0, 0), axis=d)]
    all_gather x1 -> x0, waiting for transfers between devices: 45.7 us -> none  [local(): basis_full = lax.all_gather(q_basis, 'fsdp', axis=2, tiled=True)[0]]
    all_to_all x0 -> x1, starting transfers between devices: none -> 15.4 us  [gather_over(): return jnp.concatenate(lax.all_to_all(repeated, axis, 0, 0), axis=d)]
    another operation x12 -> x13, local copies, waits for them, and re-layouts: 14.5 us -> 16.8 us
where the time goes in v1:
time: 664 us; the launch traced here: 662 us
  waiting for transfers between devices  424 us (64%)
  other arithmetic  135 us (20%)
  matrix products  28.8 us (4%)
  local copies, waits for them, and re-layouts  23.9 us (4%)
  starting transfers between devices  21.6 us (3%)
  between operations  16.5 us (2%)
  blocking collectives  12.4 us (2%)
    psum x1, waiting for transfers between devices, local(): gram = lax.psum(gram_part, 'fsdp')  138 us
    another operation x14, other arithmetic, orthonormal(): factor = jnp.linalg.cholesky(gram)  80.4 us
    reduce_scatter x1, waiting for transfers between devices, local(): lax.psum_scatter(product * scale, 'fsdp', scatter_dimension=0, tiled=True)  75 us
    psum x1, waiting for transfers between devices, local(): pmat = lax.psum(partial_left, 'tp')  72 us
    all_gather x1, waiting for transfers between devices, local(): lax.all_gather(right_b, 'fsdp', axis=0, tiled=True)  67.9 us
    all_to_all x1, waiting for transfers between devices, gather_over(): return jnp.concatenate(lax.all_to_all(repeated, axis, 0, 0), axis=d)  51.9 us
    another operation x3, other arithmetic, orthonormal(): solved = jax.scipy.linalg.solve_triangular(factor, pmat.T, lower=True).T  43.4 us
    ppermute x1, waiting for transfers between devices, extended(): lax.ppermute(lax.slice_in_dim(block, 0, width, axis=dim), axis, backward)  15.9 us
  transfers between devices with their start and end apart: 7, of which 7 were waited for; matrix products, arithmetic and copies ran while one was open for 1% of the time, Pallas kernels for 0%

profile of v1, /device:TPU:2, one launch (start us, length us, event | category | flops | bytes accessed | tf_op | source)
XLA Modules:
  0.0 662.4 jit_solution(8581217549100627083)
XLA Ops:
  7.2 2.3 stack.2
  9.5 15.4 %all-to-all-start = ((bf16[16,1,1792,32]{2,3,1,0:T(8,128)(2,1)}), bf16[16,1,1792,32]{2,3,1,0:T(8,128)(2,1)}, u32[]{:S(2)}, u32[]{:S(2)}) async-start(bf16[16,1,1792,32]{2,3,1,0:T(8,128)(2,1)} %stack.2), calls=%async_computation | async-start | bytes 3670016 | tf_op jit(solution)/shard_map/all_to_all | solution.py:12
  24.9 2.4 collective-permute-start.1
  27.4 3.4 collective-permute-start
  30.8 0.7 fusion.36
  31.5 0.6 broadcast_divide_fusion
  32.7 15.9 %collective-permute-done.1 = bf16[1,256,1792]{2,1,0:T(8,128)(2,1)S(1)} collective-permute-done((bf16[1,256,1792]{2,1,0:T(8,128)(2,1)S(1)}, bf16[1,256,1792]{2,1,0:T(8,128)(2,1)S(1)}, u32[]{:S(2)}, u32[]{:S(2)}) %collective-permute-start.1) | collective-permute-done | bytes 917536 | tf_op jit(solution)/shard_map/ppermute | solution.py:24
  48.6 3.2 collective-permute-done
  51.8 0.9 copy-done.7
  52.7 5.5 fusion.43
  58.2 51.9 %all-to-all-done = bf16[16,1,1792,32]{2,3,1,0:T(8,128)(2,1)} async-done(((bf16[16,1,1792,32]{2,3,1,0:T(8,128)(2,1)}), bf16[16,1,1792,32]{2,3,1,0:T(8,128)(2,1)}, u32[]{:S(2)}, u32[]{:S(2)}) %all-to-all-start) | async-done | bytes 1835040 | tf_op jit(solution)/shard_map/all_to_all | solution.py:12
  110.1 3.0 fusion.4
  113.2 72.0 %all-reduce.4.cloned.1.call-done = f32[256,512]{1,0:T(8,128)} async-done(((f32[256,512]{1,0:T(8,128)}), f32[256,512]{1,0:T(8,128)}) %all-reduce.4.cloned.1.call-update) | async-done | bytes 524304 | tf_op jit(solution)/shard_map/psum | solution.py:54
  185.1 3.3 fusion.46
  188.7 138.0 %all-reduce.6.cloned.1.call-done = f32[512,512]{0,1:T(8,128)} async-done(((f32[512,512]{0,1:T(8,128)}), f32[512,512]{0,1:T(8,128)}) %all-reduce.6.cloned.1.call-update) | async-done | bytes 1048592 | tf_op jit(solution)/shard_map/psum | solution.py:56
  326.7 2.6 copy.18
  329.3 1.8 fusion.3
  331.1 1.0 copy-done.4
  332.1 11.7 %cholesky.104 = f32[128,128]{1,0:T(8,128)S(1)} custom-call(f32[128,128]{1,0:T(8,128)S(1)} %cholesky.266), custom_call_target="Cholesky" | custom-call | tf_op jit(solution)/shard_map/jit(cholesky)/cholesky | solution.py:30
  343.8 1.2 cholesky.224
  345.0 9.8 %custom-call.31 = f32[1,128,128]{1,2,0:T(8,128)S(1)} custom-call(f32[1,128,128]{2,1,0:T(8,128)S(1)} %get-tuple-element.49), custom_call_target="InvertDiagBlocksLowerTriangular" | custom-call | tf_op jit(solution)/shard_map/jit(cholesky)/cholesky | solution.py:30
  354.8 2.0 constant_dynamic-update-slice_fusion.3
  356.8 1.2 convolution_subtract_fusion
  358.0 11.7 %cholesky.217 = f32[128,128]{1,0:T(8,128)S(1)} custom-call(f32[128,128]{1,0:T(8,128)S(1)} %cholesky.270), custom_call_target="Cholesky" | custom-call | tf_op jit(solution)/shard_map/jit(cholesky)/cholesky | solution.py:30
  369.7 0.6 select_reduce_fusion.2
  370.4 10.0 %custom-call.32 = f32[1,128,128]{1,2,0:T(8,128)S(1)} custom-call(f32[1,128,128]{2,1,0:T(8,128)S(1)} %get-tuple-element.46), custom_call_target="InvertDiagBlocksLowerTriangular" | custom-call | tf_op jit(solution)/shard_map/jit(cholesky)/cholesky | solution.py:30
  380.4 0.9 convolution_dynamic-update-slice_fusion
  381.3 1.4 convolution_subtract_fusion.3
  382.8 11.7 %cholesky.238 = f32[128,128]{1,0:T(8,128)S(1)} custom-call(f32[128,128]{1,0:T(8,128)S(1)} %cholesky.275), custom_call_target="Cholesky" | custom-call | tf_op jit(solution)/shard_map/jit(cholesky)/cholesky | solution.py:30
  394.5 0.6 select_reduce_fusion.1
  395.1 9.8 %custom-call.33 = f32[1,128,128]{1,2,0:T(8,128)S(1)} custom-call(f32[1,128,128]{2,1,0:T(8,128)S(1)} %get-tuple-element.43), custom_call_target="InvertDiagBlocksLowerTriangular" | custom-call | tf_op jit(solution)/shard_map/jit(cholesky)/cholesky | solution.py:30
  404.9 0.8 convolution_dynamic-update-slice_fusion.1
  405.8 1.4 convolution_subtract_fusion.5
  407.2 11.7 %cholesky.255 = f32[128,128]{1,0:T(8,128)S(1)} custom-call(f32[128,128]{1,0:T(8,128)S(1)} %convolution_subtract_fusion.5), custom_call_target="Cholesky" | custom-call | tf_op jit(solution)/shard_map/jit(cholesky)/cholesky | solution.py:30
  418.9 0.7 select_reduce_fusion
  419.6 0.7 compare_reduce_fusion.1
  420.3 0.6 compare_reduce_fusion
  420.9 0.7 compare_reduce_fusion.2
  424.1 2.6 select_select_fusion
  426.7 14.5 %while.1 = (s32[]{:T(128)}, f32[512,512]{1,0:T(8,128)}, s32[4,2]{0,1:T(2,128)S(1)}, f32[4,128,128]{2,1,0:T(8,128)}, s32[]{:T(128)}) while((s32[]{:T(128)}, f32[512,512]{1,0:T(8,128)}, s32[4,2]{0,1:T(2,128)S(1)}, f32[4,128,128]{2,1,0:T(8,128)}, s32[]{:T(128)}) %tuple.39), condition=%wide.while_cond, body=%wide.while_body.sunk | while | flops 2 | bytes 132205 | solution.py:31
  426.8 0.6 fusion.57
  427.4 3.0 bitcast_dynamic-update-slice_fusion.2
  430.4 0.6 fusion.57
  431.0 3.0 bitcast_dynamic-update-slice_fusion.2
  434.1 0.6 fusion.57
  434.7 3.0 bitcast_dynamic-update-slice_fusion.2
  437.7 0.6 fusion.57
  438.3 2.9 bitcast_dynamic-update-slice_fusion.2
  441.2 40.8 %custom-call.34 = f32[4,128,128]{1,2,0:T(8,128)} custom-call(f32[4,128,128]{2,1,0:T(8,128)} %get-tuple-element.11), custom_call_target="InvertDiagBlocksLowerTriangular" | custom-call | tf_op jit(solution)/shard_map/jit(_solve_triangular)/triangular_solve | solution.py:31
  482.0 1.1 fusion.22
  483.1 1.2 convolution_subtract_fusion.4
  484.3 1.2 fusion.30
  485.5 1.5 convolution_subtract_fusion.2
  487.0 1.2 fusion.28
  488.2 1.8 convolution_subtract_fusion.1
  490.0 1.2 fusion.27
  491.2 2.5 convolution_multiply_fusion
  493.7 75.0 %reduce-scatter.2.cloned.1.call-done = f32[32,1792]{1,0:T(8,128)} async-done(((f32[512,1792]{1,0:T(8,128)}), f32[32,1792]{1,0:T(8,128)}) %reduce-scatter.2.cloned.1.call-update) | async-done | bytes 229392 | tf_op jit(solution)/shard_map/reduce_scatter | solution.py:62
  568.7 1.1 multiply_reduce_fusion
  569.7 12.4 %psum.23 = f32[32]{0:T(128)S(1)} all-reduce(f32[32]{0:T(128)S(1)} %multiply_reduce_fusion), channel_id=1, replica_groups=mesh['rep'=4,'fsdp'=16,'tp'=8] {'tp'}, use_global_device_ids=true, to_apply=%region_14.15 | all-reduce | flops 32 | bytes 256 | tf_op jit(solution)/shard_map/psum | solution.py:63
  582.1 1.8 fusion.26
  584.0 0.8 copy.22
  584.9 67.9 %all-gather.2.cloned.1.call-done = bf16[512,1792]{1,0:T(8,128)(2,1)} async-done(((bf16[32,1792]{1,0:T(8,128)(2,1)}), bf16[512,1792]{1,0:T(8,128)(2,1)}) %all-gather.2.cloned.1.call-update) | async-done | bytes 1835024 | tf_op jit(solution)/shard_map/all_gather | solution.py:70
  652.8 3.1 fusion.2
  (39 shorter events, 1.4 us)
Async XLA Ops:
  9.5 15.4 %copy-start.5 = (bf16[1,256,1792]{2,1,0:T(8,128)(2,1)S(1)}, bf16[1,256,1792]{2,1,0:T(8,128)(2,1)}, u32[]{:S(2)}) copy-start(bf16[1,256,1792]{2,1,0:T(8,128)(2,1)} %param.5) | copy-start | bytes 2752516
  9.5 21.3 %copy-start.8 = (s32[4,3]{1,0:T(4,128)S(1)}, s32[4,3]{1,0:T(4,128)}, u32[]{:S(2)}) copy-start(s32[4,3]{1,0:T(4,128)} %param.9) | copy-start | bytes 148
  9.5 100.6 %all-to-all-start = ((bf16[16,1,1792,32]{2,3,1,0:T(8,128)(2,1)}), bf16[16,1,1792,32]{2,3,1,0:T(8,128)(2,1)}, u32[]{:S(2)}, u32[]{:S(2)}) async-start(bf16[16,1,1792,32]{2,3,1,0:T(8,128)(2,1)} %stack.2), calls=%async_computation | async-start | bytes 3670016 | tf_op jit(solution)/shard_map/all_to_all | solution.py:12
  24.9 160.3 %all-reduce.4.cloned.1.call-start = ((), (), s32[]{:S(2)}) async-start(), calls=%async_computation.2 | async-start | bytes 1048576 | tf_op jit(solution)/shard_map/psum | solution.py:54
  24.9 23.7 %collective-permute-start.1 = (bf16[1,256,1792]{2,1,0:T(8,128)(2,1)S(1)}, bf16[1,256,1792]{2,1,0:T(8,128)(2,1)S(1)}, u32[]{:S(2)}, u32[]{:S(2)}) collective-permute-start(bf16[1,256,1792]{2,1,0:T(8,128)(2,1)S(1)} %copy-done.5), channel_id=1, source_target_pairs={{128,0},{256,128},{384,256},{0,384},{129,1},{257,129},{385,257},{1... | collective-permute-start | bytes 2752520 | tf_op jit(solution)/shard_map/ppermute | solution.py:24
  27.4 24.4 %collective-permute-start = (bf16[1,256,1792]{2,1,0:T(8,128)(2,1)S(1)}, bf16[1,256,1792]{2,1,0:T(8,128)(2,1)S(1)}, u32[]{:S(2)}, u32[]{:S(2)}) collective-permute-start(bf16[1,256,1792]{2,1,0:T(8,128)(2,1)S(1)} %copy-done.5), channel_id=1, source_target_pairs={{0,128},{128,256},{256,384},{384,0},{1,129},{129,257},{257,385},{3... | collective-permute-start | bytes 2752520 | tf_op jit(solution)/shard_map/ppermute | solution.py:21
  48.6 3.2 copy-start.6
  51.8 0.9 copy-start.7
  52.7 57.4 %copy-start = (bf16[1,256,1792]{2,1,0:T(8,128)(2,1)S(1)}, bf16[1,256,1792]{2,1,0:T(8,128)(2,1)}, u32[]{:S(2)}) copy-start(bf16[1,256,1792]{2,1,0:T(8,128)(2,1)} %param.7) | copy-start | bytes 2752516
  113.1 213.6 %all-reduce.6.cloned.1.call-start = ((), (), s32[]{:S(2)}) async-start(), calls=%async_computation.3 | async-start | bytes 2097152 | tf_op jit(solution)/shard_map/psum | solution.py:56
  188.4 380.2 %reduce-scatter.2.cloned.1.call-start = ((), (), s32[]{:S(2)}) async-start(), calls=%async_computation.4 | async-start | bytes 3899392 | tf_op jit(solution)/shard_map/reduce_scatter | solution.py:62
  331.1 1.0 copy-start.4
  395.1 86.8 %copy-start.1 = (f32[256,512]{1,0:T(8,128)S(1)}, f32[256,512]{1,0:T(8,128)}, u32[]{:S(2)}) copy-start(f32[256,512]{1,0:T(8,128)} %all-reduce.4.cloned.1.call-done) | copy-start | bytes 1572868
  488.2 3.0 copy-start.2
  493.6 90.3 %copy-start.3 = (f32[128,256]{1,0:T(8,128)S(1)}, f32[128,256]{1,0:T(8,128)}, u32[]{:S(2)}) copy-start(f32[128,256]{1,0:T(8,128)} %copy-done.2) | copy-start | bytes 393220
  493.6 159.2 %all-gather.2.cloned.1.call-start = ((), (), s32[]{:S(2)}) async-start(), calls=%async_computation.5 | async-start | bytes 1949696 | tf_op jit(solution)/shard_map/all_gather | solution.py:70
Sparse Core Ops, SparseCore 0:
  113.2 71.8 all-reduce.3
  188.6 138.1 all-reduce.5
  493.8 74.8 reduce-scatter.1
  584.1 68.6 all-gather.1
